TPU v7x, 32 devices: a whole 2x2x4 slice. The times are simulated.
32 devices in a mesh: bra: 8 (over z, x), ket: 4 (over y, core).
Axes of the slice: x: 2, y: 2, z: 4, core: 2. Of those that a mesh axis runs over, the one named last changes fastest.
Arguments:
- densities: bfloat16 [8, 8, 40, 640], P('bra', 'ket'), may hold values from -6 to 6
- fit_factors: bfloat16 [8, 40, 256], replicated, may hold values from -1 to 1
- coupling: float32 [256, 256], replicated, may hold values from -0.5 to 2
- quartets: int32 [8, 4, 16, 3], P('bra', 'ket'), may hold values from 0 to 7
- live_count: int32 [8, 4], P('bra', 'ket'), may hold values from 0 to 16, as said below
Outputs:
- coulomb: bfloat16 [8, 8, 40, 640], P('bra', 'ket')
- exchange: bfloat16 [8, 8, 40, 640], P('bra', 'ket')
Inputs may be any that keep to these rules, and one draw needn't show every extreme that they name: `live_count`: the counts of two devices with the same ket index whose bra indices differ by half of the bra axis sum to 16.
All inputs are finite; a program needn't handle non-finite values.
Results may differ from a plain program's by a relative error of at most 0.007.
Values may be sent and summed in bfloat16 or wider, within the bound.
A program may use at most 64 MiB of HBM per device.

v0:
```python
import jax
import jax.numpy as jnp
from jax import lax
from jax.sharding import PartitionSpec as P


def quartet_terms(bra_left, bra_right, ket_left, ket_right, block_cd, block_bd, weight, coupling):
    single = jnp.float32
    width = bra_left.shape[0]
    dens_count = block_cd.shape[1] // width
    cube_cd = block_cd.reshape(width, width, dens_count)
    ket_image = jnp.einsum("cdk,dq->ckq", cube_cd, ket_right, preferred_element_type=single)
    fitted = jnp.sum(ket_left.astype(single)[:, None, :] * ket_image, axis=0)
    pushed = jnp.dot(fitted, coupling.T, precision=lax.Precision.HIGHEST)
    spread = (bra_left.astype(single)[:, None, :] * pushed[None, :, :]).astype(jnp.bfloat16)
    coulomb_term = jnp.einsum("akp,bp->abk", spread, bra_right, preferred_element_type=single)
    coulomb_term = (weight * coulomb_term).reshape(width, width * dens_count).astype(jnp.bfloat16)
    cube_bd = block_bd.reshape(width, width, dens_count)
    side_image = jnp.einsum(
        "bdk,dq->bkq", cube_bd, ket_right, preferred_element_type=single
    ).astype(jnp.bfloat16)
    heavy = jnp.einsum("bp,bkq->pkq", bra_right, side_image, preferred_element_type=single)
    wide = (coupling[:, None, :] * heavy).astype(jnp.bfloat16)
    narrow = jnp.einsum("ap,pkq->akq", bra_left, wide, preferred_element_type=single).astype(
        jnp.bfloat16
    )
    exchange_term = jnp.einsum("akq,cq->ack", narrow, ket_left, preferred_element_type=single)
    exchange_term = (weight * exchange_term).reshape(width, width * dens_count).astype(jnp.bfloat16)
    return (coulomb_term, exchange_term)


def per_device(densities, fit_factors, coupling, quartets, live_count):
    bra_rank = lax.axis_index("bra")
    ket_rank = lax.axis_index("ket")
    col_count = densities.shape[1]
    width = densities.shape[2]
    flat_width = densities.shape[3]
    slot_count = quartets.shape[2]
    tasks = quartets[0, 0]
    live_now = live_count[0, 0]
    second = tasks[:, 0]
    ket_first = tasks[:, 1]
    ket_second = tasks[:, 2]
    need_rows = jnp.concatenate([ket_first, second])
    need_cols = jnp.concatenate([ket_second, ket_second]) - ket_rank * col_count
    start_blocks = jnp.zeros((2 * slot_count, width, flat_width), jnp.bfloat16)
    piece = lax.all_gather(densities, "bra", axis=0, tiled=True)
    held = piece.shape[0]
    flat_piece = piece.reshape(held * col_count, width, flat_width)
    inside = (need_rows >= 0) & (need_rows < held)
    position = jnp.clip(need_rows * col_count + need_cols, 0, held * col_count - 1)
    fetched = jnp.where(inside[:, None, None], jnp.take(flat_piece, position, axis=0), start_blocks)
    block_cd = fetched[:slot_count]
    block_bd = fetched[slot_count:]
    batched_terms = jax.vmap(quartet_terms, in_axes=(0, 0, 0, 0, 0, 0, 0, None))
    slot_index = jnp.arange(slot_count, dtype=jnp.int32)
    alive = (slot_index < live_now).astype(jnp.float32)
    rows_a = jnp.full((slot_count,), bra_rank, jnp.int32)
    inputs = (
        fit_factors[rows_a],
        fit_factors[second],
        fit_factors[ket_first],
        fit_factors[ket_second],
        block_cd,
        block_bd,
        alive,
    )
    slot_total = alive.shape[0]
    group_size = 2

    def regroup(values):
        return values.reshape((slot_total // group_size, group_size) + values.shape[1:])

    grouped = jax.tree.map(regroup, inputs)

    def one_group(members):
        return batched_terms(
            members[0],
            members[1],
            members[2],
            members[3],
            members[4],
            members[5],
            members[6],
            coupling,
        )

    coul_out, exch_out = lax.map(one_group, grouped)
    coulomb_terms = coul_out.reshape((slot_total,) + coul_out.shape[2:])
    exchange_terms = exch_out.reshape((slot_total,) + exch_out.shape[2:])
    terms = jnp.concatenate([coulomb_terms, exchange_terms])
    targets = jnp.concatenate([second, ket_first])
    holder = targets // col_count
    kind_flag = jnp.concatenate(
        [jnp.zeros((slot_count,), jnp.int32), jnp.ones((slot_count,), jnp.int32)]
    )
    target_slot = kind_flag * col_count + targets % col_count
    order_out = jnp.argsort(holder, stable=True)
    arrived, arrived_slot = (
        lax.all_to_all(terms[order_out], "ket", split_axis=0, concat_axis=0, tiled=True),
        lax.all_to_all(target_slot[order_out], "ket", split_axis=0, concat_axis=0, tiled=True),
    )
    selector = (
        arrived_slot[None, :] == jnp.arange(2 * col_count, dtype=jnp.int32)[:, None]
    ).astype(jnp.bfloat16)
    summed = jnp.dot(
        selector,
        arrived.reshape(2 * slot_count, width * flat_width),
        preferred_element_type=jnp.float32,
    )
    coulomb = summed[:col_count].reshape(1, col_count, width, flat_width).astype(jnp.bfloat16)
    exchange = summed[col_count:].reshape(1, col_count, width, flat_width).astype(jnp.bfloat16)
    return (coulomb, exchange)


def solution(mesh):
    placed = (P("bra", "ket", None, None), P(), P(), P("bra", "ket", None, None), P("bra", "ket"))
    return jax.shard_map(
        per_device,
        mesh=mesh,
        in_specs=placed,
        out_specs=(P("bra", "ket", None, None), P("bra", "ket", None, None)),
        check_vma=False,
    )
```

profile of v0, /device:TPU:0, one launch (start us, length us, event | category | flops | bytes accessed | tf_op | source)
XLA Modules:
  0.0 162.5 jit_solution(1487560734440622190)
XLA Ops:
  0.6 0.7 copy.57
  1.4 0.7 fusion.39
  2.2 1.6 sort.17
  3.8 0.7 gather_fusion
  5.2 4.3 %all-to-all-start = ((s32[4,8,1]{1,2,0:T(1,128)}), s32[4,8,1]{1,2,0:T(1,128)S(1)}, u32[]{:S(2)}, u32[]{:S(2)}) async-start(s32[4,8,1]{1,2,0:T(1,128)} %bitcast.24), calls=%async_computation | async-start | bytes 4096 | tf_op jit(solution)/shard_map/all_to_all | solution.py:101
  9.6 33.0 %all_gather.3 = bf16[8,2,40,640]{3,2,1,0:T(8,128)(2,1)S(1)} all-gather(bf16[1,2,40,640]{3,2,1,0:T(8,128)(2,1)} %param.7), channel_id=1, replica_groups=mesh['bra'=8,'ket'=4] {'bra'}, dimensions={0}, use_global_device_ids=true | all-gather | bytes 921600 | tf_op jit(solution)/shard_map/all_gather | solution.py:47
  42.6 0.9 gather_fusion.4
  44.0 1.3 gather_fusion.3
  45.9 1.3 gather_fusion.2
  47.2 1.3 gather_fusion.1
  49.2 83.5 %while.12 = (s32[]{:T(128)}, bf16[8,2,40,640]{3,2,1,0:T(8,128)(2,1)}, bf16[8,2,40,640]{3,2,1,0:T(8,128)(2,1)}, f32[8,2]{1,0:T(8,128)S(1)}, bf16[8,2,40,256]{3,2,...) while((s32[]{:T(128)}, ...), condition=%wide.region_3.4_spmd, body=%wide.region_1.3_spmd.sunk | while | flops 471965696 | bytes 9874657 | solution.py:88
  50.2 2.8 %fusion.83 = bf16[2,40,16,256]{3,1,2,0:T(8,128)(2,1)S(1)} fusion(f32[256,256]{1,0:T(8,128)S(1)} %get-tuple-element.250, bf16[2,40,16,256]{3,2,1,0:T(8,128)(2,1)S(1)} %convolution_convert_fusion.3, bf16[8,2,40,256]{3,2,1,0:T(8,128)(2,1)} %get-tuple-element.246, s32[]{:T(128)} %get-tuple-element.229, bf16[8,2,40,256]{3,2,1,0:T(8,128)(2,1)} %get-tuple-element.245), kind=kOutput, calls=%fused_computation.12.clone.1 | convolution fusion | flops 340066304 | bytes 1655808 | tf_op jit(solution)/shard_map/while/body/eval_jaxpr/vmap(ap,pkq->akq)/dot_general | solution.py:24
  53.0 1.3 fusion.85
  55.9 0.8 bitcast_convert_fusion.3
  57.4 1.3 fusion.88
  60.7 2.8 %fusion.83 = bf16[2,40,16,256]{3,1,2,0:T(8,128)(2,1)S(1)} fusion(f32[256,256]{1,0:T(8,128)S(1)} %get-tuple-element.250, bf16[2,40,16,256]{3,2,1,0:T(8,128)(2,1)S(1)} %convolution_convert_fusion.3, bf16[8,2,40,256]{3,2,1,0:T(8,128)(2,1)} %get-tuple-element.246, s32[]{:T(128)} %get-tuple-element.229, bf16[8,2,40,256]{3,2,1,0:T(8,128)(2,1)} %get-tuple-element.245), kind=kOutput, calls=%fused_computation.12.clone.1 | convolution fusion | flops 340066304 | bytes 1655808 | tf_op jit(solution)/shard_map/while/body/eval_jaxpr/vmap(ap,pkq->akq)/dot_general | solution.py:24
  63.5 1.3 fusion.85
  66.4 0.8 bitcast_convert_fusion.3
  67.9 1.3 fusion.88
  71.1 2.8 %fusion.83 = bf16[2,40,16,256]{3,1,2,0:T(8,128)(2,1)S(1)} fusion(f32[256,256]{1,0:T(8,128)S(1)} %get-tuple-element.250, bf16[2,40,16,256]{3,2,1,0:T(8,128)(2,1)S(1)} %convolution_convert_fusion.3, bf16[8,2,40,256]{3,2,1,0:T(8,128)(2,1)} %get-tuple-element.246, s32[]{:T(128)} %get-tuple-element.229, bf16[8,2,40,256]{3,2,1,0:T(8,128)(2,1)} %get-tuple-element.245), kind=kOutput, calls=%fused_computation.12.clone.1 | convolution fusion | flops 340066304 | bytes 1655808 | tf_op jit(solution)/shard_map/while/body/eval_jaxpr/vmap(ap,pkq->akq)/dot_general | solution.py:24
  73.9 1.3 fusion.85
  76.8 0.8 bitcast_convert_fusion.3
  78.3 1.3 fusion.88
  81.5 2.8 %fusion.83 = bf16[2,40,16,256]{3,1,2,0:T(8,128)(2,1)S(1)} fusion(f32[256,256]{1,0:T(8,128)S(1)} %get-tuple-element.250, bf16[2,40,16,256]{3,2,1,0:T(8,128)(2,1)S(1)} %convolution_convert_fusion.3, bf16[8,2,40,256]{3,2,1,0:T(8,128)(2,1)} %get-tuple-element.246, s32[]{:T(128)} %get-tuple-element.229, bf16[8,2,40,256]{3,2,1,0:T(8,128)(2,1)} %get-tuple-element.245), kind=kOutput, calls=%fused_computation.12.clone.1 | convolution fusion | flops 340066304 | bytes 1655808 | tf_op jit(solution)/shard_map/while/body/eval_jaxpr/vmap(ap,pkq->akq)/dot_general | solution.py:24
  84.4 1.3 fusion.85
  87.3 0.8 bitcast_convert_fusion.3
  88.8 1.3 fusion.88
  92.0 2.8 %fusion.83 = bf16[2,40,16,256]{3,1,2,0:T(8,128)(2,1)S(1)} fusion(f32[256,256]{1,0:T(8,128)S(1)} %get-tuple-element.250, bf16[2,40,16,256]{3,2,1,0:T(8,128)(2,1)S(1)} %convolution_convert_fusion.3, bf16[8,2,40,256]{3,2,1,0:T(8,128)(2,1)} %get-tuple-element.246, s32[]{:T(128)} %get-tuple-element.229, bf16[8,2,40,256]{3,2,1,0:T(8,128)(2,1)} %get-tuple-element.245), kind=kOutput, calls=%fused_computation.12.clone.1 | convolution fusion | flops 340066304 | bytes 1655808 | tf_op jit(solution)/shard_map/while/body/eval_jaxpr/vmap(ap,pkq->akq)/dot_general | solution.py:24
  94.8 1.3 fusion.85
  97.7 0.8 bitcast_convert_fusion.3
  99.2 1.3 fusion.88
  102.4 2.8 %fusion.83 = bf16[2,40,16,256]{3,1,2,0:T(8,128)(2,1)S(1)} fusion(f32[256,256]{1,0:T(8,128)S(1)} %get-tuple-element.250, bf16[2,40,16,256]{3,2,1,0:T(8,128)(2,1)S(1)} %convolution_convert_fusion.3, bf16[8,2,40,256]{3,2,1,0:T(8,128)(2,1)} %get-tuple-element.246, s32[]{:T(128)} %get-tuple-element.229, bf16[8,2,40,256]{3,2,1,0:T(8,128)(2,1)} %get-tuple-element.245), kind=kOutput, calls=%fused_computation.12.clone.1 | convolution fusion | flops 340066304 | bytes 1655808 | tf_op jit(solution)/shard_map/while/body/eval_jaxpr/vmap(ap,pkq->akq)/dot_general | solution.py:24
  105.2 1.3 fusion.85
  106.8 0.7 constant_dynamic-update-slice_fusion.4
  108.1 0.8 bitcast_convert_fusion.3
  109.6 1.3 fusion.88
  112.9 2.8 %fusion.83 = bf16[2,40,16,256]{3,1,2,0:T(8,128)(2,1)S(1)} fusion(f32[256,256]{1,0:T(8,128)S(1)} %get-tuple-element.250, bf16[2,40,16,256]{3,2,1,0:T(8,128)(2,1)S(1)} %convolution_convert_fusion.3, bf16[8,2,40,256]{3,2,1,0:T(8,128)(2,1)} %get-tuple-element.246, s32[]{:T(128)} %get-tuple-element.229, bf16[8,2,40,256]{3,2,1,0:T(8,128)(2,1)} %get-tuple-element.245), kind=kOutput, calls=%fused_computation.12.clone.1 | convolution fusion | flops 340066304 | bytes 1655808 | tf_op jit(solution)/shard_map/while/body/eval_jaxpr/vmap(ap,pkq->akq)/dot_general | solution.py:24
  115.7 1.3 fusion.85
  118.6 0.8 bitcast_convert_fusion.3
  120.1 1.3 fusion.88
  123.3 2.8 %fusion.83 = bf16[2,40,16,256]{3,1,2,0:T(8,128)(2,1)S(1)} fusion(f32[256,256]{1,0:T(8,128)S(1)} %get-tuple-element.250, bf16[2,40,16,256]{3,2,1,0:T(8,128)(2,1)S(1)} %convolution_convert_fusion.3, bf16[8,2,40,256]{3,2,1,0:T(8,128)(2,1)} %get-tuple-element.246, s32[]{:T(128)} %get-tuple-element.229, bf16[8,2,40,256]{3,2,1,0:T(8,128)(2,1)} %get-tuple-element.245), kind=kOutput, calls=%fused_computation.12.clone.1 | convolution fusion | flops 340066304 | bytes 1655808 | tf_op jit(solution)/shard_map/while/body/eval_jaxpr/vmap(ap,pkq->akq)/dot_general | solution.py:24
  126.1 1.3 fusion.85
  129.0 0.8 bitcast_convert_fusion.3
  130.5 1.3 fusion.88
  132.7 1.6 pad_maximum_fusion
  134.2 1.9 %gather_fusion.6 = bf16[32,40,640]{2,1,0:T(8,128)(2,1)} fusion(bf16[32,40,640]{2,1,0:T(8,128)(2,1)S(1)} %pad_maximum_fusion, s32[1024]{0:T(1024)S(1)} %pad_clamp_fusion.5), kind=kCustom, calls=%fused_computation.6 | custom fusion | bytes 3276928 | tf_op jit(solution)/shard_map/gather | solution.py:100
  136.2 3.6 %all-to-all-start.1 = ((bf16[32,40,640]{2,1,0:T(8,128)(2,1)}), bf16[32,40,640]{2,1,0:T(8,128)(2,1)S(1)}, u32[]{:S(2)}, u32[]{:S(2)}) async-start(bf16[32,40,640]{2,1,0:T(8,128)(2,1)} %gather_fusion.6), calls=%async_computation.1 | async-start | bytes 3276800 | tf_op jit(solution)/shard_map/all_to_all | solution.py:100
  141.0 19.5 %all-to-all-done.1 = bf16[32,40,640]{2,1,0:T(8,128)(2,1)S(1)} async-done(((bf16[32,40,640]{2,1,0:T(8,128)(2,1)}), bf16[32,40,640]{2,1,0:T(8,128)(2,1)S(1)}, u32[]{:S(2)}, u32[]{:S(2)}) %all-to-all-start.1) | async-done | bytes 1638432 | tf_op jit(solution)/shard_map/all_to_all | solution.py:100
  (183 shorter events, 37.3 us)
Async XLA Ops:
  0.6 43.4 %copy-start = (bf16[8,40,256]{2,1,0:T(8,128)(2,1)S(1)}, bf16[8,40,256]{2,1,0:T(8,128)(2,1)}, u32[]{:S(2)}) copy-start(bf16[8,40,256]{2,1,0:T(8,128)(2,1)} %param.8) | copy-start | bytes 491524
  5.2 131.0 %all-to-all-start = ((s32[4,8,1]{1,2,0:T(1,128)}), s32[4,8,1]{1,2,0:T(1,128)S(1)}, u32[]{:S(2)}, u32[]{:S(2)}) async-start(s32[4,8,1]{1,2,0:T(1,128)} %bitcast.24), calls=%async_computation | async-start | bytes 4096 | tf_op jit(solution)/shard_map/all_to_all | solution.py:101
  44.0 5.2 %copy-start.1 = (f32[256,256]{1,0:T(8,128)S(1)}, f32[256,256]{1,0:T(8,128)}, u32[]{:S(2)}) copy-start(f32[256,256]{1,0:T(8,128)} %param.9) | copy-start | bytes 786436
  49.2 1.0 copy-start.2
  54.4 2.4 %copy-start.3 = (bf16[8,2,40,256]{3,2,1,0:T(8,128)(2,1)S(1)}, bf16[8,2,40,256]{3,2,1,0:T(8,128)(2,1)}, u32[]{:S(2)}) copy-start(bf16[8,2,40,256]{3,2,1,0:T(8,128)(2,1)} %copy-done.2) | copy-start | bytes 983044 | tf_op jit(solution)/shard_map/while
  59.6 1.0 copy-start.2
  64.8 2.4 %copy-start.3 = (bf16[8,2,40,256]{3,2,1,0:T(8,128)(2,1)S(1)}, bf16[8,2,40,256]{3,2,1,0:T(8,128)(2,1)}, u32[]{:S(2)}) copy-start(bf16[8,2,40,256]{3,2,1,0:T(8,128)(2,1)} %copy-done.2) | copy-start | bytes 983044 | tf_op jit(solution)/shard_map/while
  70.1 1.0 copy-start.2
  75.2 2.4 %copy-start.3 = (bf16[8,2,40,256]{3,2,1,0:T(8,128)(2,1)S(1)}, bf16[8,2,40,256]{3,2,1,0:T(8,128)(2,1)}, u32[]{:S(2)}) copy-start(bf16[8,2,40,256]{3,2,1,0:T(8,128)(2,1)} %copy-done.2) | copy-start | bytes 983044 | tf_op jit(solution)/shard_map/while
  80.5 1.0 copy-start.2
  85.7 2.4 %copy-start.3 = (bf16[8,2,40,256]{3,2,1,0:T(8,128)(2,1)S(1)}, bf16[8,2,40,256]{3,2,1,0:T(8,128)(2,1)}, u32[]{:S(2)}) copy-start(bf16[8,2,40,256]{3,2,1,0:T(8,128)(2,1)} %copy-done.2) | copy-start | bytes 983044 | tf_op jit(solution)/shard_map/while
  91.0 1.0 copy-start.2
  96.1 2.4 %copy-start.3 = (bf16[8,2,40,256]{3,2,1,0:T(8,128)(2,1)S(1)}, bf16[8,2,40,256]{3,2,1,0:T(8,128)(2,1)}, u32[]{:S(2)}) copy-start(bf16[8,2,40,256]{3,2,1,0:T(8,128)(2,1)} %copy-done.2) | copy-start | bytes 983044 | tf_op jit(solution)/shard_map/while
  101.4 1.0 copy-start.2
  106.6 2.4 %copy-start.3 = (bf16[8,2,40,256]{3,2,1,0:T(8,128)(2,1)S(1)}, bf16[8,2,40,256]{3,2,1,0:T(8,128)(2,1)}, u32[]{:S(2)}) copy-start(bf16[8,2,40,256]{3,2,1,0:T(8,128)(2,1)} %copy-done.2) | copy-start | bytes 983044 | tf_op jit(solution)/shard_map/while
  111.8 1.0 copy-start.2
  117.0 2.4 %copy-start.3 = (bf16[8,2,40,256]{3,2,1,0:T(8,128)(2,1)S(1)}, bf16[8,2,40,256]{3,2,1,0:T(8,128)(2,1)}, u32[]{:S(2)}) copy-start(bf16[8,2,40,256]{3,2,1,0:T(8,128)(2,1)} %copy-done.2) | copy-start | bytes 983044 | tf_op jit(solution)/shard_map/while
  122.3 1.0 copy-start.2
  127.4 2.4 %copy-start.3 = (bf16[8,2,40,256]{3,2,1,0:T(8,128)(2,1)S(1)}, bf16[8,2,40,256]{3,2,1,0:T(8,128)(2,1)}, u32[]{:S(2)}) copy-start(bf16[8,2,40,256]{3,2,1,0:T(8,128)(2,1)} %copy-done.2) | copy-start | bytes 983044 | tf_op jit(solution)/shard_map/while
  136.2 24.3 %all-to-all-start.1 = ((bf16[32,40,640]{2,1,0:T(8,128)(2,1)}), bf16[32,40,640]{2,1,0:T(8,128)(2,1)S(1)}, u32[]{:S(2)}, u32[]{:S(2)}) async-start(bf16[32,40,640]{2,1,0:T(8,128)(2,1)} %gather_fusion.6), calls=%async_computation.1 | async-start | bytes 3276800 | tf_op jit(solution)/shard_map/all_to_all | solution.py:100
where the time goes:
time: 165 us; the launch traced here: 162 us
  matrix products  51.3 us (31%)
  local copies, waits for them, and re-layouts  36.7 us (22%)
  blocking collectives  33 us (20%)
  waiting for transfers between devices  19.5 us (12%)
  other arithmetic  11.8 us (7%)
  starting transfers between devices  7.83 us (5%)
    all_gather x1, blocking collectives, per_device(): piece = lax.all_gather(densities, 'bra', axis=0, tiled=True)  33 us
    dot_general x8, matrix products, quartet_terms(): jnp.einsum('ap,pkq->akq', bra_left, wide, preferred_element_type=single)  22.3 us
    all_to_all x1, waiting for transfers between devices, per_device(): lax.all_to_all(terms[order_out], 'ket', split_axis=0, concat_axis=0, tile...  19.5 us
    dynamic_update_slice x32, local copies, waits for them, and re-layouts, per_device(): coul_out, exch_out = lax.map(one_group, grouped)  13.2 us
    dot_general x8, matrix products, quartet_terms(): jnp.einsum('akp,bp->abk', spread, bra_right, preferred_element_type=single)  10.5 us
    dot_general x8, matrix products, quartet_terms(): jnp.einsum('akq,cq->ack', narrow, ket_left, preferred_element_type=single)  10.5 us
    convert_element_type x8, other arithmetic, quartet_terms(): fitted = jnp.sum(ket_left.astype(single)[:, None, :] * ket_image, axis=0)  6.55 us
    all_to_all x1, starting transfers between devices, per_device(): lax.all_to_all(target_slot[order_out], 'ket', split_axis=0, concat_axis=0...  4.26 us
  transfers between devices with their start and end apart: 2, of which 1 were waited for; matrix products, arithmetic and copies ran while one was open for 57% of the time, Pallas kernels for 0%

commit v1 on v0

v1 whole, which is shorter than its diff:
```python
import functools

import jax
import jax.numpy as jnp
from jax import lax
from jax.experimental import pallas as pl
from jax.experimental.pallas import tpu as pltpu
from jax.sharding import PartitionSpec as P

MESH = pl.DeviceIdType.MESH


def kernel(dims, tasks_ref, live_ref, dens_ref, fit_ref, coup_ref, coul_ref, exch_ref,
           held, counts, factor, trans, image, inner, spread, term_out, term_in, fit_out, fit_in,
           hold_send, hold_recv, term_send, term_recv, fit_send, fit_recv):
    n_bra, n_ket, cols, width, dens_count, points, blocks, slots = dims
    flat = width * dens_count
    lanes = 128
    single, half = jnp.float32, jnp.bfloat16
    bra, ket = lax.axis_index("bra"), lax.axis_index("ket")

    barrier = pltpu.get_barrier_semaphore()
    for step in range(1, n_bra):
        pl.semaphore_signal(barrier, inc=1, device_id=(lax.rem(bra + step, n_bra), ket), device_id_type=MESH)
    for step in range(1, n_ket):
        pl.semaphore_signal(barrier, inc=1, device_id=(bra, lax.rem(ket + step, n_ket)), device_id_type=MESH)
    pl.semaphore_wait(barrier, n_bra + n_ket - 2)

    def hold_copy(step):
        return pltpu.make_async_remote_copy(
            src_ref=dens_ref, dst_ref=held.at[bra], send_sem=hold_send.at[step - 1],
            recv_sem=hold_recv.at[step - 1], device_id=(lax.rem(bra + step, n_bra), ket), device_id_type=MESH)

    for step in range(1, n_bra):
        hold_copy(step).start()
    held[pl.ds(bra, 1)] = dens_ref[...][None]

    live = live_ref[0, 0]
    codes = []
    for t in range(slots):
        code = (tasks_ref[0, 0, t, 0] * blocks + tasks_ref[0, 0, t, 1]) * cols + tasks_ref[0, 0, t, 2] - ket * cols
        codes.append(jnp.where(t < live, code, -1))
    span = blocks * cols

    def count_rows(first, carry):
        rows = lax.broadcasted_iota(jnp.int32, (span, points), 0) + first * span
        total = jnp.zeros((span, points), single)
        for code in codes:
            total += jnp.where(rows == code, 1.0, 0.0)
        counts[pl.ds(pl.multiple_of(first * span, 8), span), :] = total
        return carry

    lax.fori_loop(0, blocks, count_rows, 0)
    for blk in range(blocks):
        factor[blk * width:(blk + 1) * width, :] = fit_ref[blk].astype(single)
    bra_t = jnp.transpose(jnp.concatenate([fit_ref[bra].astype(single), jnp.zeros((lanes - width, points), single)], axis=0)).astype(half)
    ket_f = [fit_ref[ket * cols + d].astype(single) for d in range(cols)]
    pad = -(cols * width) % lanes
    ket_t = jnp.transpose(jnp.concatenate(ket_f + [jnp.zeros((pad, points), single)], axis=0)).astype(half)[:, :cols * width]
    coup_t = jnp.transpose(coup_ref[...])

    for step in range(1, n_bra):
        hold_copy(step).wait_recv()

    for d in range(cols):
        whole = jnp.concatenate([held[blk, d].astype(single) for blk in range(blocks)], axis=0)
        trans[d] = jnp.transpose(whole).astype(half)

    def one_target(s, carry):
        target = lax.rem((ket + 1) * cols + s, blocks)
        fitted = jnp.zeros((dens_count, points), single)
        for d in range(cols):
            mixed = []
            for blk in range(blocks):
                g = factor[blk * width:(blk + 1) * width, :]
                side = counts[pl.ds((blk * blocks + target) * cols + d, 1), :]
                direct = counts[pl.ds((target * blocks + blk) * cols + d, 1), :]
                mixed.append(jnp.concatenate([g * side, g * direct], axis=1))
            weights = jnp.concatenate(mixed, axis=0).astype(half)
            both = jnp.dot(trans[d], weights, preferred_element_type=single)
            for h in range(points // lanes):
                image[d * (points // lanes) + h] = both[:, h * lanes:(h + 1) * lanes]
            cube = both[:, points:].reshape(width, dens_count, points)
            fitted += jnp.sum(cube * ket_f[d][:, None, :], axis=0)
        fit_out[s] = fitted
        g_target = fit_ref[target]
        for k in range(dens_count):
            u_k = jnp.concatenate([
                jnp.concatenate([
                    image[d * (points // lanes) + h, pl.ds(k, width, stride=dens_count), :]
                    for h in range(points // lanes)], axis=1)
                for d in range(cols)], axis=0)
            heavy = jnp.dot(ket_t, u_k.astype(half), preferred_element_type=single)
            wide = (heavy * coup_t).astype(half)
            inner[k * width:(k + 1) * width, :] = jnp.dot(g_target, wide, preferred_element_type=single)
        last = jnp.dot(inner[...].astype(half), bra_t, preferred_element_type=single)
        for k in range(dens_count):
            spread[pl.ds(k, width, stride=dens_count), :] = last[k * width:(k + 1) * width, :]
        term_out[s] = jnp.transpose(spread[...])[:width].astype(half)
        return carry

    def term_copy(s):
        dest = (bra, lax.rem(ket + 1 + s // cols, n_ket))
        return (
            pltpu.make_async_remote_copy(
                src_ref=term_out.at[s], dst_ref=term_in.at[s], send_sem=term_send.at[s],
                recv_sem=term_recv.at[s], device_id=dest, device_id_type=MESH),
            pltpu.make_async_remote_copy(
                src_ref=fit_out.at[s], dst_ref=fit_in.at[s], send_sem=fit_send.at[s],
                recv_sem=fit_recv.at[s], device_id=dest, device_id_type=MESH),
        )

    away = blocks - cols

    def step_body(s, carry):
        one_target(s, 0)

        @pl.when(s < away)
        def _():
            for copy in term_copy(s):
                copy.start()
        return carry

    lax.fori_loop(0, blocks, step_body, 0)

    for s in range(away):
        for copy in term_copy(s):
            copy.wait_recv()
    for y in range(cols):
        exch = term_out[away + y].astype(single)
        fitted = fit_out[away + y]
        for other in range(n_ket - 1):
            exch += term_in[other * cols + y].astype(single)
            fitted += fit_in[other * cols + y]
        exch_ref[y] = exch.astype(half)
        pushed = jnp.dot(fitted, coup_t, precision=lax.Precision.HIGHEST, preferred_element_type=single)
        g_right = fit_ref[ket * cols + y].astype(single)
        rows = (g_right[:, None, :] * pushed[None, :, :]).reshape(flat, points).astype(half)
        out = jnp.dot(rows, bra_t, preferred_element_type=single)
        coul_ref[y] = jnp.transpose(out)[:width].astype(half)

    for step in range(1, n_bra):
        hold_copy(step).wait_send()
    for s in range(away):
        for copy in term_copy(s):
            copy.wait_send()


def per_device(n_bra, n_ket, densities, fit_factors, coupling, quartets, live_count):
    cols, width, flat = densities.shape[1:]
    blocks, points = fit_factors.shape[0], fit_factors.shape[2]
    slots = quartets.shape[2]
    dens_count = flat // width
    dims = (n_bra, n_ket, cols, width, dens_count, points, blocks, slots)
    single, half = jnp.float32, jnp.bfloat16
    away = blocks - cols
    vmem = pl.BlockSpec(memory_space=pltpu.VMEM)
    smem = pl.BlockSpec(memory_space=pltpu.SMEM)
    out = jax.ShapeDtypeStruct((cols, width, flat), half)
    dma = pltpu.SemaphoreType.DMA
    coulomb, exchange = pl.pallas_call(
        functools.partial(kernel, dims),
        out_shape=(out, out),
        in_specs=[smem, smem, vmem, vmem, vmem],
        out_specs=(vmem, vmem),
        scratch_shapes=[
            pltpu.VMEM((n_bra, cols, width, flat), half),
            pltpu.VMEM((blocks * blocks * cols, points), single),
            pltpu.VMEM((blocks * width, points), single),
            pltpu.VMEM((cols, flat, blocks * width), half),
            pltpu.VMEM((cols * (points // 128), flat, 128), single),
            pltpu.VMEM((flat, points), single),
            pltpu.VMEM((flat, 128), single),
            pltpu.VMEM((blocks, width, flat), half),
            pltpu.VMEM((away, width, flat), half),
            pltpu.VMEM((blocks, dens_count, points), single),
            pltpu.VMEM((away, dens_count, points), single),
            dma((n_bra - 1,)), dma((n_bra - 1,)), dma((away,)), dma((away,)), dma((away,)), dma((away,)),
        ],
        compiler_params=pltpu.CompilerParams(collective_id=0, has_side_effects=True, vmem_limit_bytes=56 * 1024 * 1024),
    )(quartets, live_count, densities[0], fit_factors, coupling)
    return coulomb[None], exchange[None]


def solution(mesh):
    placed = (P("bra", "ket", None, None), P(), P(), P("bra", "ket", None, None), P("bra", "ket"))
    return jax.shard_map(
        functools.partial(per_device, mesh.shape["bra"], mesh.shape["ket"]),
        mesh=mesh,
        in_specs=placed,
        out_specs=(P("bra", "ket", None, None), P("bra", "ket", None, None)),
        check_vma=False,
    )
```

time: 165 us -> 67.8 us (0.41)
  the two profiles are of different devices: /device:TPU:0 before, /device:TPU:15 now
where the time goes in v1:
time: 67.8 us; the launch traced here: 67.7 us
  Pallas kernels  63.4 us (94%)
  local copies, waits for them, and re-layouts  2.92 us (4%)
  between operations  1.31 us (2%)
    pallas_call x1, Pallas kernels, per_device(): pl.pallas_call(functools.partial(kernel, dims), out_shape=(out, out), in_...  63.4 us
    unnamed x7, local copies, waits for them, and re-layouts  2.92 us

profile of v1, /device:TPU:15, one launch (start us, length us, event | category | flops | bytes accessed | tf_op | source)
XLA Modules:
  0.0 67.7 jit_solution(7733487520955746131)
XLA Ops:
  0.6 0.0 copy-start.1
  1.3 0.0 copy-done.1
  1.3 0.7 %copy.7.tasks_ref = s32[1,1,16,3]{3,2,1,0:T(8,128)} copy(s32[1,1,16,3]{2,1,3,0:T(1,128)S(1)} %copy-done.1) | data formatting | bytes 384 | tf_op args[3]
  2.0 63.4 %shard_map.68 = (bf16[2,40,640]{2,1,0:T(8,128)(2,1)}, bf16[2,40,640]{2,1,0:T(8,128)(2,1)}) custom-call(s32[1,1,16,3]{3,2,1,0:T(8,128)} %copy.7.tasks_ref, s32[1,1]{1,0:T(1,128)S(6)} %copy.10.live_ref, bf16[2,40,640]{2,1,0:T(8,128)(2,1)} %bitcast.3, bf16[8,40,256]{2,1,0:T(8,128)(2,1)} %fit_ref.1, f32[256,256]{1,0:T(8,128)} %coup_ref.1), custom_call_target="tpu_custom_call" | custom-call | tf_op jit(solution)/shard_map/pallas_call | solution.py:161
  65.4 0.0 copy-start
  65.4 1.6 %copy.11 = bf16[1,2,40,640]{3,2,1,0:T(8,128)(2,1)} copy(bf16[1,2,40,640]{3,2,1,0:T(8,128)(2,1)} %bitcast.5) | data formatting | bytes 204800
  67.0 0.0 copy-done
  67.0 0.6 copy.12
Async XLA Ops:
  0.6 0.7 %copy-start.1 = (s32[1,1,16,3]{2,1,3,0:T(1,128)S(1)}, s32[1,1,16,3]{2,1,3,0:T(1,128)}, u32[]{:S(2)}) copy-start(s32[1,1,16,3]{2,1,3,0:T(1,128)} %param.8) | copy-start | bytes 580
  65.4 1.6 %copy-start = (bf16[2,40,640]{2,1,0:T(8,128)(2,1)S(1)}, bf16[2,40,640]{2,1,0:T(8,128)(2,1)}, u32[]{:S(2)}) copy-start(bf16[2,40,640]{2,1,0:T(8,128)(2,1)} %get-tuple-element.5) | copy-start | bytes 307204

commit v2 on v1

v2 whole, which is shorter than its diff:
```python
import functools

import jax
import jax.numpy as jnp
from jax import lax
from jax.experimental import pallas as pl
from jax.experimental.pallas import tpu as pltpu
from jax.sharding import PartitionSpec as P

MESH = pl.DeviceIdType.MESH


def kernel(dims, tasks_ref, live_ref, dens_ref, fit_ref, coup_ref, coul_ref, exch_ref,
           held, image, stack, fits, wide, inner, spread, term_out, term_in, fit_out, fit_in,
           far_send, far_recv, pair_send, pair_recv, term_send, term_recv, fit_send, fit_recv):
    n_bra, n_ket, cols, width, dens_count, points, blocks, slots, named, padded = dims
    flat = width * dens_count
    lanes = 128
    halves = points // lanes
    single, half = jnp.float32, jnp.bfloat16
    bra, ket = lax.axis_index("bra"), lax.axis_index("ket")
    n_far = n_bra // 2
    far, near = bra // 2, bra % 2
    partner = far * 2 + (1 - near)

    def far_dev(step):
        return (lax.rem(far + step, n_far) * 2 + near, ket)

    def ket_dev(m):
        return (bra, lax.rem(ket + m, n_ket))

    barrier = pltpu.get_barrier_semaphore()
    for step in range(1, n_far):
        pl.semaphore_signal(barrier, inc=1, device_id=far_dev(step), device_id_type=MESH)
    pl.semaphore_signal(barrier, inc=1, device_id=(partner, ket), device_id_type=MESH)
    for m in range(1, n_ket):
        pl.semaphore_signal(barrier, inc=1, device_id=ket_dev(m), device_id_type=MESH)
    pl.semaphore_wait(barrier, n_far + n_ket - 1)

    def far_copy(step):
        return pltpu.make_async_remote_copy(
            src_ref=dens_ref, dst_ref=held.at[bra], send_sem=far_send.at[step - 1],
            recv_sem=far_recv.at[step - 1], device_id=far_dev(step), device_id_type=MESH)

    def column_block(step):
        return lax.rem(far - step + n_far, n_far) * 2

    def pair_copy(step):
        block = column_block(step) + near
        return pltpu.make_async_remote_copy(
            src_ref=held.at[block], dst_ref=held.at[block], send_sem=pair_send.at[step],
            recv_sem=pair_recv.at[step], device_id=(partner, ket), device_id_type=MESH)

    first_copy = pltpu.make_async_remote_copy(
        src_ref=dens_ref, dst_ref=held.at[bra], send_sem=pair_send.at[0],
        recv_sem=pair_recv.at[0], device_id=(partner, ket), device_id_type=MESH)
    first_copy.start()
    for step in range(1, n_far):
        far_copy(step).start()
    held[pl.ds(bra, 1)] = dens_ref[...][None]

    live = live_ref[0, 0]
    rows_b = [tasks_ref[0, 0, t, 0] for t in range(slots)]
    rows_c = [tasks_ref[0, 0, t, 1] for t in range(slots)]
    cols_d = [tasks_ref[0, 0, t, 2] - ket * cols for t in range(slots)]

    def keys_of(rows):
        keys = []
        for t in range(slots):
            rank = jnp.int32(0)
            for before in range(t):
                rank = rank + jnp.where(rows[before] == rows[t], 1, 0)
            keys.append(jnp.where(t < live, rows[t] * named + rank, -1))
        return keys

    keys_b, keys_c = keys_of(rows_b), keys_of(rows_c)
    pairs_b = [rows_b[t] * cols + cols_d[t] + 1 for t in range(slots)]
    pairs_c = [rows_c[t] * cols + cols_d[t] + 1 for t in range(slots)]

    def find(keys, values, want):
        found = jnp.int32(0)
        for t in range(slots):
            found = found + jnp.where(keys[t] == want, values[t], 0)
        return jnp.maximum(found - 1, 0), jnp.where(found > 0, 1.0, 0.0)

    bra_t = jnp.transpose(jnp.concatenate([fit_ref[bra].astype(single), jnp.zeros((lanes - width, points), single)], axis=0)).astype(half)
    ket_f = [fit_ref[ket * cols + d].astype(single) for d in range(cols)]
    coup_t = jnp.transpose(coup_ref[...])

    def process(block):
        for d in range(cols):
            both = lax.dot_general(held[block, d], fit_ref[block], (((0,), (0,)), ((), ())), preferred_element_type=single)
            fits[block * cols + d] = jnp.sum(both.reshape(width, dens_count, points) * ket_f[d][:, None, :], axis=0)
            for h in range(halves):
                image[d * halves + h] = both[:, h * lanes:(h + 1) * lanes]
            for k in range(dens_count):
                part = jnp.concatenate([image[d * halves + h, pl.ds(k, width, stride=dens_count), :] for h in range(halves)], axis=1)
                part = jnp.concatenate([part, jnp.zeros((padded - width, points), single)], axis=0)
                stack[block * cols + d, k] = part.astype(half)

    def gather_step(step, carry):
        @pl.when(step > 0)
        def _():
            far_copy(step).wait_recv()
            pair_copy(step).start()
        process(column_block(step) + near)

        @pl.when(step > 0)
        def _():
            pair_copy(step - 1).wait_recv()
            process(column_block(step - 1) + 1 - near)
        return carry

    lax.fori_loop(0, n_far, gather_step, 0)
    pair_copy(n_far - 1).wait_recv()
    process(column_block(n_far - 1) + 1 - near)

    def holder_of(m):
        return lax.rem(ket + m, n_ket)

    def fit_copy(m):
        return pltpu.make_async_remote_copy(
            src_ref=fit_out.at[m], dst_ref=fit_in.at[m - 1], send_sem=fit_send.at[m - 1],
            recv_sem=fit_recv.at[m - 1], device_id=ket_dev(m), device_id_type=MESH)

    def fit_target(s, carry):
        target = holder_of(1 + s // cols) * cols + s % cols
        total = jnp.zeros((dens_count, points), single)
        for n in range(named):
            at, scale = find(keys_b, pairs_c, target * named + n)
            total += fits[at] * scale
        fit_out[lax.rem(1 + s // cols, n_ket), s % cols] = total
        return carry

    lax.fori_loop(0, blocks, fit_target, 0)
    for m in range(1, n_ket):
        fit_copy(m).start()

    def one_target(s):
        target = holder_of(1 + s // cols) * cols + s % cols
        found = [find(keys_c, pairs_b, target * named + n) for n in range(named)]
        right = []
        for at, scale in found:
            right.append(fit_ref[ket * cols + lax.rem(at, cols)].astype(single) * scale)
            right.append(jnp.zeros((padded - width, points), single))
        depth = named * padded
        right.append(jnp.zeros((-depth % lanes, points), single))
        right_t = jnp.transpose(jnp.concatenate(right, axis=0)).astype(half)[:, :depth]
        for k in range(dens_count):
            left = jnp.concatenate([stack[at, k] for at, _ in found], axis=0)
            heavy = jnp.dot(right_t, left, preferred_element_type=single)
            wide[:, k * points:(k + 1) * points] = (heavy * coup_t).astype(half)
        g_target = fit_ref[target]
        for k in range(dens_count):
            inner[k * width:(k + 1) * width, :] = jnp.dot(
                g_target, wide[:, k * points:(k + 1) * points], preferred_element_type=single)
        last = jnp.dot(inner[...].astype(half), bra_t, preferred_element_type=single)
        for k in range(dens_count):
            spread[pl.ds(k, width, stride=dens_count), :] = last[k * width:(k + 1) * width, :]
        term_out[s] = jnp.transpose(spread[...])[:width].astype(half)

    def term_copy(s):
        return pltpu.make_async_remote_copy(
            src_ref=term_out.at[s], dst_ref=term_in.at[s], send_sem=term_send.at[s],
            recv_sem=term_recv.at[s], device_id=ket_dev(1 + s // cols), device_id_type=MESH)

    away = blocks - cols

    def step_body(s, carry):
        one_target(s)

        @pl.when(s < away)
        def _():
            term_copy(s).start()
        return carry

    lax.fori_loop(0, blocks, step_body, 0)

    for m in range(1, n_ket):
        fit_copy(m).wait_recv()
    for y in range(cols):
        fitted = fit_out[0, y]
        for other in range(n_ket - 1):
            fitted += fit_in[other, y]
        pushed = jnp.dot(fitted, coup_t, precision=lax.Precision.HIGHEST, preferred_element_type=single)
        g_right = fit_ref[ket * cols + y].astype(single)
        rows = (g_right[:, None, :] * pushed[None, :, :]).reshape(flat, points).astype(half)
        out = jnp.dot(rows, bra_t, preferred_element_type=single)
        coul_ref[y] = jnp.transpose(out)[:width].astype(half)
    for s in range(away):
        term_copy(s).wait_recv()
    for y in range(cols):
        exch = term_out[away + y].astype(single)
        for other in range(n_ket - 1):
            exch += term_in[other * cols + y].astype(single)
        exch_ref[y] = exch.astype(half)

    for step in range(1, n_far):
        far_copy(step).wait_send()
    first_copy.wait_send()
    for step in range(1, n_far):
        pair_copy(step).wait_send()
    for m in range(1, n_ket):
        fit_copy(m).wait_send()
    for s in range(away):
        term_copy(s).wait_send()


def per_device(n_bra, n_ket, densities, fit_factors, coupling, quartets, live_count):
    cols, width, flat = densities.shape[1:]
    blocks, points = fit_factors.shape[0], fit_factors.shape[2]
    slots = quartets.shape[2]
    dens_count = flat // width
    named = 2 * slots // blocks
    padded = -(-width // 16) * 16
    dims = (n_bra, n_ket, cols, width, dens_count, points, blocks, slots, named, padded)
    single, half = jnp.float32, jnp.bfloat16
    away = blocks - cols
    vmem = pl.BlockSpec(memory_space=pltpu.VMEM)
    smem = pl.BlockSpec(memory_space=pltpu.SMEM)
    out = jax.ShapeDtypeStruct((cols, width, flat), half)
    dma = pltpu.SemaphoreType.DMA
    coulomb, exchange = pl.pallas_call(
        functools.partial(kernel, dims),
        out_shape=(out, out),
        in_specs=[smem, smem, vmem, vmem, vmem],
        out_specs=(vmem, vmem),
        scratch_shapes=[
            pltpu.VMEM((n_bra, cols, width, flat), half),
            pltpu.VMEM((cols * (points // 128), flat, 128), single),
            pltpu.VMEM((blocks * cols, dens_count, padded, points), half),
            pltpu.VMEM((blocks * cols, dens_count, points), single),
            pltpu.VMEM((points, dens_count * points), half),
            pltpu.VMEM((flat, points), single),
            pltpu.VMEM((flat, 128), single),
            pltpu.VMEM((blocks, width, flat), half),
            pltpu.VMEM((away, width, flat), half),
            pltpu.VMEM((n_ket, cols, dens_count, points), single),
            pltpu.VMEM((n_ket - 1, cols, dens_count, points), single),
            dma((n_bra // 2 - 1,)), dma((n_bra // 2 - 1,)), dma((n_bra // 2,)), dma((n_bra // 2,)),
            dma((away,)), dma((away,)), dma((n_ket - 1,)), dma((n_ket - 1,)),
        ],
        compiler_params=pltpu.CompilerParams(collective_id=0, has_side_effects=True, vmem_limit_bytes=56 * 1024 * 1024),
    )(quartets, live_count, densities[0], fit_factors, coupling)
    return coulomb[None], exchange[None]


def solution(mesh):
    placed = (P("bra", "ket", None, None), P(), P(), P("bra", "ket", None, None), P("bra", "ket"))
    return jax.shard_map(
        functools.partial(per_device, mesh.shape["bra"], mesh.shape["ket"]),
        mesh=mesh,
        in_specs=placed,
        out_specs=(P("bra", "ket", None, None), P("bra", "ket", None, None)),
        check_vma=False,
    )
```

time: 67.8 us -> 41.1 us (0.61)
  the two profiles are of different devices: /device:TPU:15 before, /device:TPU:0 now
where the time goes in v2:
time: 41.1 us; the launch traced here: 40.9 us
  Pallas kernels  36.7 us (89%)
  local copies, waits for them, and re-layouts  2.92 us (7%)
  between operations  1.31 us (3%)
    pallas_call x1, Pallas kernels, per_device(): pl.pallas_call(functools.partial(kernel, dims), out_shape=(out, out), in_...  36.7 us
    unnamed x7, local copies, waits for them, and re-layouts  2.92 us

profile of v2, /device:TPU:0, one launch (start us, length us, event | category | flops | bytes accessed | tf_op | source)
XLA Modules:
  0.0 40.9 jit_solution(8907849677117778301)
XLA Ops:
  0.6 0.0 copy-start.1
  1.3 0.0 copy-done.1
  1.3 0.7 %copy.7.tasks_ref = s32[1,1,16,3]{3,2,1,0:T(8,128)} copy(s32[1,1,16,3]{2,1,3,0:T(1,128)S(1)} %copy-done.1) | data formatting | bytes 384 | tf_op args[3]
  2.0 36.7 %shard_map.68 = (bf16[2,40,640]{2,1,0:T(8,128)(2,1)}, bf16[2,40,640]{2,1,0:T(8,128)(2,1)}) custom-call(s32[1,1,16,3]{3,2,1,0:T(8,128)} %copy.7.tasks_ref, s32[1,1]{1,0:T(1,128)S(6)} %copy.10.live_ref, bf16[2,40,640]{2,1,0:T(8,128)(2,1)} %bitcast.3, bf16[8,40,256]{2,1,0:T(8,128)(2,1)} %fit_ref.1, f32[256,256]{1,0:T(8,128)} %coup_ref.1), custom_call_target="tpu_custom_call" | custom-call | tf_op jit(solution)/shard_map/pallas_call | solution.py:223
  38.7 0.0 copy-start
  38.7 1.6 %copy.11 = bf16[1,2,40,640]{3,2,1,0:T(8,128)(2,1)} copy(bf16[1,2,40,640]{3,2,1,0:T(8,128)(2,1)} %bitcast.5) | data formatting | bytes 204800
  40.2 0.0 copy-done
  40.3 0.6 %copy.12 = bf16[1,2,40,640]{3,2,1,0:T(8,128)(2,1)} copy(bf16[1,2,40,640]{3,2,1,0:T(8,128)(2,1)S(1)} %bitcast.4) | data formatting | bytes 204800
Async XLA Ops:
  0.6 0.7 %copy-start.1 = (s32[1,1,16,3]{2,1,3,0:T(1,128)S(1)}, s32[1,1,16,3]{2,1,3,0:T(1,128)}, u32[]{:S(2)}) copy-start(s32[1,1,16,3]{2,1,3,0:T(1,128)} %param.8) | copy-start | bytes 580
  38.7 1.6 %copy-start = (bf16[2,40,640]{2,1,0:T(8,128)(2,1)S(1)}, bf16[2,40,640]{2,1,0:T(8,128)(2,1)}, u32[]{:S(2)}) copy-start(bf16[2,40,640]{2,1,0:T(8,128)(2,1)} %get-tuple-element.5) | copy-start | bytes 307204

commit v3 on v2

--- a/solution.py
+++ b/solution.py
@@ -12,7 +12,8 @@
 
 def kernel(dims, tasks_ref, live_ref, dens_ref, fit_ref, coup_ref, coul_ref, exch_ref,
            held, image, stack, fits, wide, inner, spread, term_out, term_in, fit_out, fit_in,
-           far_send, far_recv, pair_send, pair_recv, term_send, term_recv, fit_send, fit_recv):
+           right_all, pick_b, pick_c, gain_b,
+           up_send, up_recv, down_send, down_recv, pair_send, pair_recv, term_send, term_recv, fit_send, fit_recv):
     n_bra, n_ket, cols, width, dens_count, points, blocks, slots, named, padded = dims
     flat = width * dens_count
     lanes = 128
@@ -23,46 +24,80 @@
     far, near = bra // 2, bra % 2
     partner = far * 2 + (1 - near)
 
-    def far_dev(step):
-        return (lax.rem(far + step, n_far) * 2 + near, ket)
-
     def ket_dev(m):
         return (bra, lax.rem(ket + m, n_ket))
 
     barrier = pltpu.get_barrier_semaphore()
-    for step in range(1, n_far):
-        pl.semaphore_signal(barrier, inc=1, device_id=far_dev(step), device_id_type=MESH)
+    has_up, has_down = far + 1 < n_far, far > 0
+
+    @pl.when(has_up)
+    def _():
+        pl.semaphore_signal(barrier, inc=1, device_id=(bra + 2, ket), device_id_type=MESH)
+
+    @pl.when(has_down)
+    def _():
+        pl.semaphore_signal(barrier, inc=1, device_id=(bra - 2, ket), device_id_type=MESH)
+
     pl.semaphore_signal(barrier, inc=1, device_id=(partner, ket), device_id_type=MESH)
     for m in range(1, n_ket):
         pl.semaphore_signal(barrier, inc=1, device_id=ket_dev(m), device_id_type=MESH)
-    pl.semaphore_wait(barrier, n_far + n_ket - 1)
-
-    def far_copy(step):
-        return pltpu.make_async_remote_copy(
-            src_ref=dens_ref, dst_ref=held.at[bra], send_sem=far_send.at[step - 1],
-            recv_sem=far_recv.at[step - 1], device_id=far_dev(step), device_id_type=MESH)
-
-    def column_block(step):
-        return lax.rem(far - step + n_far, n_far) * 2
-
-    def pair_copy(step):
-        block = column_block(step) + near
-        return pltpu.make_async_remote_copy(
-            src_ref=held.at[block], dst_ref=held.at[block], send_sem=pair_send.at[step],
-            recv_sem=pair_recv.at[step], device_id=(partner, ket), device_id_type=MESH)
+    pl.semaphore_wait(barrier, n_ket + jnp.minimum(n_far - 1 - far, 1) + jnp.minimum(far, 1))
+
+    def up_copy(dist, src=None):
+        block = bra - 2 * dist
+        return pltpu.make_async_remote_copy(
+            src_ref=held.at[block] if src is None else src, dst_ref=held.at[block], send_sem=up_send.at[dist],
+            recv_sem=up_recv.at[dist], device_id=(bra + 2, ket), device_id_type=MESH)
+
+    def down_copy(dist, src=None):
+        block = bra + 2 * dist
+        return pltpu.make_async_remote_copy(
+            src_ref=held.at[block] if src is None else src, dst_ref=held.at[block], send_sem=down_send.at[dist],
+            recv_sem=down_recv.at[dist], device_id=(bra - 2, ket), device_id_type=MESH)
+
+    def pair_copy(row):
+        block = row * 2 + near
+        return pltpu.make_async_remote_copy(
+            src_ref=held.at[block], dst_ref=held.at[block], send_sem=pair_send.at[row],
+            recv_sem=pair_recv.at[row], device_id=(partner, ket), device_id_type=MESH)
+
+    def pair_wait(row):
+        block = row * 2 + 1 - near
+        pltpu.make_async_remote_copy(
+            src_ref=held.at[block], dst_ref=held.at[block], send_sem=pair_send.at[row],
+            recv_sem=pair_recv.at[row], device_id=(partner, ket), device_id_type=MESH).wait_recv()
+
+    def up_wait(dist):
+        block = bra - 2 * dist
+        pltpu.make_async_remote_copy(
+            src_ref=held.at[block], dst_ref=held.at[block], send_sem=up_send.at[dist - 1],
+            recv_sem=up_recv.at[dist - 1], device_id=(bra - 2, ket), device_id_type=MESH).wait_recv()
+
+    def down_wait(dist):
+        block = bra + 2 * dist
+        pltpu.make_async_remote_copy(
+            src_ref=held.at[block], dst_ref=held.at[block], send_sem=down_send.at[dist - 1],
+            recv_sem=down_recv.at[dist - 1], device_id=(bra + 2, ket), device_id_type=MESH).wait_recv()
 
     first_copy = pltpu.make_async_remote_copy(
-        src_ref=dens_ref, dst_ref=held.at[bra], send_sem=pair_send.at[0],
-        recv_sem=pair_recv.at[0], device_id=(partner, ket), device_id_type=MESH)
+        src_ref=dens_ref, dst_ref=held.at[bra], send_sem=pair_send.at[far],
+        recv_sem=pair_recv.at[far], device_id=(partner, ket), device_id_type=MESH)
     first_copy.start()
-    for step in range(1, n_far):
-        far_copy(step).start()
+
+    @pl.when(has_up)
+    def _():
+        up_copy(0, dens_ref).start()
+
+    @pl.when(has_down)
+    def _():
+        down_copy(0, dens_ref).start()
+
     held[pl.ds(bra, 1)] = dens_ref[...][None]
 
     live = live_ref[0, 0]
-    rows_b = [tasks_ref[0, 0, t, 0] for t in range(slots)]
-    rows_c = [tasks_ref[0, 0, t, 1] for t in range(slots)]
-    cols_d = [tasks_ref[0, 0, t, 2] - ket * cols for t in range(slots)]
+    rows_b = [tasks_ref[0, 0, 0, t] for t in range(slots)]
+    rows_c = [tasks_ref[0, 1, 0, t] for t in range(slots)]
+    cols_d = [tasks_ref[0, 2, 0, t] - ket * cols for t in range(slots)]
 
     def keys_of(rows):
         keys = []
@@ -86,6 +121,26 @@
     bra_t = jnp.transpose(jnp.concatenate([fit_ref[bra].astype(single), jnp.zeros((lanes - width, points), single)], axis=0)).astype(half)
     ket_f = [fit_ref[ket * cols + d].astype(single) for d in range(cols)]
     coup_t = jnp.transpose(coup_ref[...])
+
+    def holder_of(m):
+        return lax.rem(ket + m, n_ket)
+
+    depth = named * padded
+
+    def list_target(s, carry):
+        target = holder_of(1 + s // cols) * cols + s % cols
+        right = []
+        for n in range(named):
+            at, scale = find(keys_b, pairs_c, target * named + n)
+            pick_b[s, n] = at
+            gain_b[s, n] = scale
+            at, scale = find(keys_c, pairs_b, target * named + n)
+            pick_c[s, n] = at
+            right.append(fit_ref[ket * cols + lax.rem(at, cols)].astype(single) * scale)
+            right.append(jnp.zeros((padded - width, points), single))
+        right.append(jnp.zeros((-depth % lanes, points), single))
+        right_all[s] = jnp.transpose(jnp.concatenate(right, axis=0)).astype(half)
+        return carry
 
     def process(block):
         for d in range(cols):
@@ -98,25 +153,45 @@
                 part = jnp.concatenate([part, jnp.zeros((padded - width, points), single)], axis=0)
                 stack[block * cols + d, k] = part.astype(half)
 
-    def gather_step(step, carry):
-        @pl.when(step > 0)
-        def _():
-            far_copy(step).wait_recv()
-            pair_copy(step).start()
-        process(column_block(step) + near)
-
-        @pl.when(step > 0)
-        def _():
-            pair_copy(step - 1).wait_recv()
-            process(column_block(step - 1) + 1 - near)
+    lax.fori_loop(0, blocks, list_target, 0)
+
+    def gather_step(dist, carry):
+        below, above = far - dist, far + dist
+
+        @pl.when(below >= 0)
+        def _():
+            @pl.when(dist > 0)
+            def _():
+                up_wait(dist)
+                pair_copy(below).start()
+
+                @pl.when(has_up)
+                def _():
+                    up_copy(dist).start()
+
+        @pl.when((above < n_far) & (dist > 0))
+        def _():
+            down_wait(dist)
+            pair_copy(above).start()
+
+            @pl.when(has_down)
+            def _():
+                down_copy(dist).start()
+
+        @pl.when(below >= 0)
+        def _():
+            process(below * 2 + near)
+            pair_wait(below)
+            process(below * 2 + 1 - near)
+
+        @pl.when((above < n_far) & (dist > 0))
+        def _():
+            process(above * 2 + near)
+            pair_wait(above)
+            process(above * 2 + 1 - near)
         return carry
 
     lax.fori_loop(0, n_far, gather_step, 0)
-    pair_copy(n_far - 1).wait_recv()
-    process(column_block(n_far - 1) + 1 - near)
-
-    def holder_of(m):
-        return lax.rem(ket + m, n_ket)
 
     def fit_copy(m):
         return pltpu.make_async_remote_copy(
@@ -124,11 +199,9 @@
             recv_sem=fit_recv.at[m - 1], device_id=ket_dev(m), device_id_type=MESH)
 
     def fit_target(s, carry):
-        target = holder_of(1 + s // cols) * cols + s % cols
         total = jnp.zeros((dens_count, points), single)
         for n in range(named):
-            at, scale = find(keys_b, pairs_c, target * named + n)
-            total += fits[at] * scale
+            total += fits[pick_b[s, n]] * gain_b[s, n]
         fit_out[lax.rem(1 + s // cols, n_ket), s % cols] = total
         return carry
 
@@ -138,16 +211,10 @@
 
     def one_target(s):
         target = holder_of(1 + s // cols) * cols + s % cols
-        found = [find(keys_c, pairs_b, target * named + n) for n in range(named)]
-        right = []
-        for at, scale in found:
-            right.append(fit_ref[ket * cols + lax.rem(at, cols)].astype(single) * scale)
-            right.append(jnp.zeros((padded - width, points), single))
-        depth = named * padded
-        right.append(jnp.zeros((-depth % lanes, points), single))
-        right_t = jnp.transpose(jnp.concatenate(right, axis=0)).astype(half)[:, :depth]
+        found = [pick_c[s, n] for n in range(named)]
+        right_t = right_all[s][:, :depth]
         for k in range(dens_count):
-            left = jnp.concatenate([stack[at, k] for at, _ in found], axis=0)
+            left = jnp.concatenate([stack[at, k] for at in found], axis=0)
             heavy = jnp.dot(right_t, left, preferred_element_type=single)
             wide[:, k * points:(k + 1) * points] = (heavy * coup_t).astype(half)
         g_target = fit_ref[target]
@@ -195,11 +262,27 @@
             exch += term_in[other * cols + y].astype(single)
         exch_ref[y] = exch.astype(half)
 
-    for step in range(1, n_far):
-        far_copy(step).wait_send()
     first_copy.wait_send()
-    for step in range(1, n_far):
-        pair_copy(step).wait_send()
+
+    def drain(dist, carry):
+        @pl.when((far - dist >= 0) & has_up)
+        def _():
+            up_copy(dist).wait_send()
+
+        @pl.when((far + dist < n_far) & has_down)
+        def _():
+            down_copy(dist).wait_send()
+
+        @pl.when((far - dist >= 0) & (dist > 0))
+        def _():
+            pair_copy(far - dist).wait_send()
+
+        @pl.when((far + dist < n_far) & (dist > 0))
+        def _():
+            pair_copy(far + dist).wait_send()
+        return carry
+
+    lax.fori_loop(0, n_far, drain, 0)
     for m in range(1, n_ket):
         fit_copy(m).wait_send()
     for s in range(away):
@@ -237,11 +320,16 @@
             pltpu.VMEM((away, width, flat), half),
             pltpu.VMEM((n_ket, cols, dens_count, points), single),
             pltpu.VMEM((n_ket - 1, cols, dens_count, points), single),
-            dma((n_bra // 2 - 1,)), dma((n_bra // 2 - 1,)), dma((n_bra // 2,)), dma((n_bra // 2,)),
+            pltpu.VMEM((blocks, points, -(-named * padded // 128) * 128), half),
+            pltpu.SMEM((blocks, named), jnp.int32),
+            pltpu.SMEM((blocks, named), jnp.int32),
+            pltpu.SMEM((blocks, named), single),
+            dma((n_bra // 2,)), dma((n_bra // 2,)), dma((n_bra // 2,)), dma((n_bra // 2,)),
+            dma((n_bra // 2,)), dma((n_bra // 2,)),
             dma((away,)), dma((away,)), dma((n_ket - 1,)), dma((n_ket - 1,)),
         ],
         compiler_params=pltpu.CompilerParams(collective_id=0, has_side_effects=True, vmem_limit_bytes=56 * 1024 * 1024),
-    )(quartets, live_count, densities[0], fit_factors, coupling)
+    )(jnp.transpose(quartets, (0, 3, 1, 2)), live_count, densities[0], fit_factors, coupling)
     return coulomb[None], exchange[None]
 
 

time: 41.1 us -> 41.9 us (1.019)
  Pallas kernels: 36.7 us -> 38.2 us
  local copies, waits for them, and re-layouts: 2.92 us -> 2.23 us
    pallas_call x1, Pallas kernels: 36.7 us -> 38.2 us  [per_device(): pl.pallas_call(functools.partial(kernel, dims), out_shape=(out, out), in_...]
    unnamed x7 -> x4, local copies, waits for them, and re-layouts: 2.92 us -> 2.23 us
where the time goes in v3:
time: 41.9 us; the launch traced here: 41.7 us
  Pallas kernels  38.2 us (91%)
  local copies, waits for them, and re-layouts  2.23 us (5%)
  between operations  1.29 us (3%)
    pallas_call x1, Pallas kernels, per_device(): pl.pallas_call(functools.partial(kernel, dims), out_shape=(out, out), in_...  38.2 us
    unnamed x4, local copies, waits for them, and re-layouts  2.23 us

profile of v3, /device:TPU:0, one launch (start us, length us, event | category | flops | bytes accessed | tf_op | source)
XLA Modules:
  0.0 41.7 jit_solution(4932806051760539674)
XLA Ops:
  1.3 38.2 %shard_map.68 = (bf16[2,40,640]{2,1,0:T(8,128)(2,1)}, bf16[2,40,640]{2,1,0:T(8,128)(2,1)}) custom-call(s32[1,3,1,16]{3,2,1,0:T(1,128)} %bitcast.7, s32[1,1]{1,0:T(1,128)S(6)} %copy.9.live_ref, bf16[2,40,640]{2,1,0:T(8,128)(2,1)} %bitcast.6, bf16[8,40,256]{2,1,0:T(8,128)(2,1)} %fit_ref.1, f32[256,256]{1,0:T(8,128)} %coup_ref.1), custom_call_target="tpu_custom_call" | custom-call | tf_op jit(solution)/shard_map/pallas_call | solution.py:306
  39.5 0.0 copy-start
  39.5 1.6 %copy.10 = bf16[1,2,40,640]{3,2,1,0:T(8,128)(2,1)} copy(bf16[1,2,40,640]{3,2,1,0:T(8,128)(2,1)} %bitcast.5) | data formatting | bytes 204800
  41.1 0.0 copy-done
  41.1 0.6 %copy.11 = bf16[1,2,40,640]{3,2,1,0:T(8,128)(2,1)} copy(bf16[1,2,40,640]{3,2,1,0:T(8,128)(2,1)S(1)} %bitcast.4) | data formatting | bytes 204800
Async XLA Ops:
  39.5 1.6 %copy-start = (bf16[2,40,640]{2,1,0:T(8,128)(2,1)S(1)}, bf16[2,40,640]{2,1,0:T(8,128)(2,1)}, u32[]{:S(2)}) copy-start(bf16[2,40,640]{2,1,0:T(8,128)(2,1)} %get-tuple-element.5) | copy-start | bytes 307204

commit v4 on v2

--- a/solution.py
+++ b/solution.py
@@ -12,6 +12,7 @@
 
 def kernel(dims, tasks_ref, live_ref, dens_ref, fit_ref, coup_ref, coul_ref, exch_ref,
            held, image, stack, fits, wide, inner, spread, term_out, term_in, fit_out, fit_in,
+           right_all, pick_b, pick_c, gain_b,
            far_send, far_recv, pair_send, pair_recv, term_send, term_recv, fit_send, fit_recv):
     n_bra, n_ket, cols, width, dens_count, points, blocks, slots, named, padded = dims
     flat = width * dens_count
@@ -37,6 +38,11 @@
         pl.semaphore_signal(barrier, inc=1, device_id=ket_dev(m), device_id_type=MESH)
     pl.semaphore_wait(barrier, n_far + n_ket - 1)
 
+    def order(at):
+        if isinstance(at, int):
+            return (at + 1) // 2 if at % 2 else (n_far - at // 2) % n_far
+        return jnp.where(at % 2 == 1, (at + 1) // 2, (n_far - at // 2) % n_far)
+
     def far_copy(step):
         return pltpu.make_async_remote_copy(
             src_ref=dens_ref, dst_ref=held.at[bra], send_sem=far_send.at[step - 1],
@@ -55,14 +61,15 @@
         src_ref=dens_ref, dst_ref=held.at[bra], send_sem=pair_send.at[0],
         recv_sem=pair_recv.at[0], device_id=(partner, ket), device_id_type=MESH)
     first_copy.start()
-    for step in range(1, n_far):
+
+    for step in [order(at) for at in range(1, n_far)]:
         far_copy(step).start()
     held[pl.ds(bra, 1)] = dens_ref[...][None]
 
     live = live_ref[0, 0]
-    rows_b = [tasks_ref[0, 0, t, 0] for t in range(slots)]
-    rows_c = [tasks_ref[0, 0, t, 1] for t in range(slots)]
-    cols_d = [tasks_ref[0, 0, t, 2] - ket * cols for t in range(slots)]
+    rows_b = [tasks_ref[0, 0, 0, t] for t in range(slots)]
+    rows_c = [tasks_ref[0, 1, 0, t] for t in range(slots)]
+    cols_d = [tasks_ref[0, 2, 0, t] - ket * cols for t in range(slots)]
 
     def keys_of(rows):
         keys = []
@@ -86,6 +93,26 @@
     bra_t = jnp.transpose(jnp.concatenate([fit_ref[bra].astype(single), jnp.zeros((lanes - width, points), single)], axis=0)).astype(half)
     ket_f = [fit_ref[ket * cols + d].astype(single) for d in range(cols)]
     coup_t = jnp.transpose(coup_ref[...])
+
+    def holder_of(m):
+        return lax.rem(ket + m, n_ket)
+
+    depth = named * padded
+
+    def list_target(s, carry):
+        target = holder_of(1 + s // cols) * cols + s % cols
+        right = []
+        for n in range(named):
+            at, scale = find(keys_b, pairs_c, target * named + n)
+            pick_b[s, n] = at
+            gain_b[s, n] = scale
+            at, scale = find(keys_c, pairs_b, target * named + n)
+            pick_c[s, n] = at
+            right.append(fit_ref[ket * cols + lax.rem(at, cols)].astype(single) * scale)
+            right.append(jnp.zeros((padded - width, points), single))
+        right.append(jnp.zeros((-depth % lanes, points), single))
+        right_all[s] = jnp.transpose(jnp.concatenate(right, axis=0)).astype(half)
+        return carry
 
     def process(block):
         for d in range(cols):
@@ -98,25 +125,27 @@
                 part = jnp.concatenate([part, jnp.zeros((padded - width, points), single)], axis=0)
                 stack[block * cols + d, k] = part.astype(half)
 
-    def gather_step(step, carry):
-        @pl.when(step > 0)
+    lax.fori_loop(0, blocks, list_target, 0)
+
+    def gather_step(at, carry):
+        step = order(at)
+
+        @pl.when(at > 0)
         def _():
             far_copy(step).wait_recv()
             pair_copy(step).start()
         process(column_block(step) + near)
 
-        @pl.when(step > 0)
+        @pl.when(at > 0)
         def _():
-            pair_copy(step - 1).wait_recv()
-            process(column_block(step - 1) + 1 - near)
+            past = order(at - 1)
+            pair_copy(past).wait_recv()
+            process(column_block(past) + 1 - near)
         return carry
 
     lax.fori_loop(0, n_far, gather_step, 0)
-    pair_copy(n_far - 1).wait_recv()
-    process(column_block(n_far - 1) + 1 - near)
-
-    def holder_of(m):
-        return lax.rem(ket + m, n_ket)
+    pair_copy(order(n_far - 1)).wait_recv()
+    process(column_block(order(n_far - 1)) + 1 - near)
 
     def fit_copy(m):
         return pltpu.make_async_remote_copy(
@@ -124,11 +153,9 @@
             recv_sem=fit_recv.at[m - 1], device_id=ket_dev(m), device_id_type=MESH)
 
     def fit_target(s, carry):
-        target = holder_of(1 + s // cols) * cols + s % cols
         total = jnp.zeros((dens_count, points), single)
         for n in range(named):
-            at, scale = find(keys_b, pairs_c, target * named + n)
-            total += fits[at] * scale
+            total += fits[pick_b[s, n]] * gain_b[s, n]
         fit_out[lax.rem(1 + s // cols, n_ket), s % cols] = total
         return carry
 
@@ -138,16 +165,10 @@
 
     def one_target(s):
         target = holder_of(1 + s // cols) * cols + s % cols
-        found = [find(keys_c, pairs_b, target * named + n) for n in range(named)]
-        right = []
-        for at, scale in found:
-            right.append(fit_ref[ket * cols + lax.rem(at, cols)].astype(single) * scale)
-            right.append(jnp.zeros((padded - width, points), single))
-        depth = named * padded
-        right.append(jnp.zeros((-depth % lanes, points), single))
-        right_t = jnp.transpose(jnp.concatenate(right, axis=0)).astype(half)[:, :depth]
+        found = [pick_c[s, n] for n in range(named)]
+        right_t = right_all[s][:, :depth]
         for k in range(dens_count):
-            left = jnp.concatenate([stack[at, k] for at, _ in found], axis=0)
+            left = jnp.concatenate([stack[at, k] for at in found], axis=0)
             heavy = jnp.dot(right_t, left, preferred_element_type=single)
             wide[:, k * points:(k + 1) * points] = (heavy * coup_t).astype(half)
         g_target = fit_ref[target]
@@ -237,11 +258,15 @@
             pltpu.VMEM((away, width, flat), half),
             pltpu.VMEM((n_ket, cols, dens_count, points), single),
             pltpu.VMEM((n_ket - 1, cols, dens_count, points), single),
+            pltpu.VMEM((blocks, points, -(-named * padded // 128) * 128), half),
+            pltpu.SMEM((blocks, named), jnp.int32),
+            pltpu.SMEM((blocks, named), jnp.int32),
+            pltpu.SMEM((blocks, named), single),
             dma((n_bra // 2 - 1,)), dma((n_bra // 2 - 1,)), dma((n_bra // 2,)), dma((n_bra // 2,)),
             dma((away,)), dma((away,)), dma((n_ket - 1,)), dma((n_ket - 1,)),
         ],
         compiler_params=pltpu.CompilerParams(collective_id=0, has_side_effects=True, vmem_limit_bytes=56 * 1024 * 1024),
-    )(quartets, live_count, densities[0], fit_factors, coupling)
+    )(jnp.transpose(quartets, (0, 3, 1, 2)), live_count, densities[0], fit_factors, coupling)
     return coulomb[None], exchange[None]
 
 

time: 41.1 us -> 37.9 us (0.922)
  Pallas kernels: 36.7 us -> 34.2 us
  local copies, waits for them, and re-layouts: 2.92 us -> 2.23 us
    pallas_call x1, Pallas kernels: 36.7 us -> 34.2 us  [per_device(): pl.pallas_call(functools.partial(kernel, dims), out_shape=(out, out), in_...]
    unnamed x7 -> x4, local copies, waits for them, and re-layouts: 2.92 us -> 2.23 us
where the time goes in v4:
time: 37.9 us; the launch traced here: 37.7 us
  Pallas kernels  34.2 us (90%)
  local copies, waits for them, and re-layouts  2.23 us (6%)
  between operations  1.29 us (3%)
    pallas_call x1, Pallas kernels, per_device(): pl.pallas_call(functools.partial(kernel, dims), out_shape=(out, out), in_...  34.2 us
    unnamed x4, local copies, waits for them, and re-layouts  2.23 us

profile of v4, /device:TPU:0, one launch (start us, length us, event | category | flops | bytes accessed | tf_op | source)
XLA Modules:
  0.0 37.7 jit_solution(10199774808276216496)
XLA Ops:
  1.3 34.2 %shard_map.68 = (bf16[2,40,640]{2,1,0:T(8,128)(2,1)}, bf16[2,40,640]{2,1,0:T(8,128)(2,1)}) custom-call(s32[1,3,1,16]{3,2,1,0:T(1,128)} %bitcast.7, s32[1,1]{1,0:T(1,128)S(6)} %copy.9.live_ref, bf16[2,40,640]{2,1,0:T(8,128)(2,1)} %bitcast.6, bf16[8,40,256]{2,1,0:T(8,128)(2,1)} %fit_ref.1, f32[256,256]{1,0:T(8,128)} %coup_ref.1), custom_call_target="tpu_custom_call" | custom-call | tf_op jit(solution)/shard_map/pallas_call | solution.py:244
  35.5 0.0 copy-start
  35.5 1.6 %copy.10 = bf16[1,2,40,640]{3,2,1,0:T(8,128)(2,1)} copy(bf16[1,2,40,640]{3,2,1,0:T(8,128)(2,1)} %bitcast.5) | data formatting | bytes 204800
  37.1 0.0 copy-done
  37.1 0.6 %copy.11 = bf16[1,2,40,640]{3,2,1,0:T(8,128)(2,1)} copy(bf16[1,2,40,640]{3,2,1,0:T(8,128)(2,1)S(1)} %bitcast.4) | data formatting | bytes 204800
Async XLA Ops:
  35.5 1.6 %copy-start = (bf16[2,40,640]{2,1,0:T(8,128)(2,1)S(1)}, bf16[2,40,640]{2,1,0:T(8,128)(2,1)}, u32[]{:S(2)}) copy-start(bf16[2,40,640]{2,1,0:T(8,128)(2,1)} %get-tuple-element.5) | copy-start | bytes 307204

commit v5 on v4

--- a/solution.py
+++ b/solution.py
@@ -10,9 +10,9 @@
 MESH = pl.DeviceIdType.MESH
 
 
-def kernel(dims, tasks_ref, live_ref, dens_ref, fit_ref, coup_ref, coul_ref, exch_ref,
+def kernel(dims, tasks_ref, live_ref, dens_ref, fit_hbm, coup_hbm, coul_ref, exch_ref,
            held, image, stack, fits, wide, inner, spread, term_out, term_in, fit_out, fit_in,
-           right_all, pick_b, pick_c, gain_b,
+           fit_ref, coup_ref, load_sem, right_all, pick_b, pick_c, gain_b,
            far_send, far_recv, pair_send, pair_recv, term_send, term_recv, fit_send, fit_recv):
     n_bra, n_ket, cols, width, dens_count, points, blocks, slots, named, padded = dims
     flat = width * dens_count
@@ -30,6 +30,13 @@
     def ket_dev(m):
         return (bra, lax.rem(ket + m, n_ket))
 
+    loads = (
+        pltpu.make_async_copy(dens_ref, held.at[bra], load_sem.at[0]),
+        pltpu.make_async_copy(fit_hbm, fit_ref, load_sem.at[1]),
+        pltpu.make_async_copy(coup_hbm, coup_ref, load_sem.at[2]),
+    )
+    for load in loads:
+        load.start()
     barrier = pltpu.get_barrier_semaphore()
     for step in range(1, n_far):
         pl.semaphore_signal(barrier, inc=1, device_id=far_dev(step), device_id_type=MESH)
@@ -64,7 +71,8 @@
 
     for step in [order(at) for at in range(1, n_far)]:
         far_copy(step).start()
-    held[pl.ds(bra, 1)] = dens_ref[...][None]
+    for load in loads:
+        load.wait()
 
     live = live_ref[0, 0]
     rows_b = [tasks_ref[0, 0, 0, t] for t in range(slots)]
@@ -244,7 +252,7 @@
     coulomb, exchange = pl.pallas_call(
         functools.partial(kernel, dims),
         out_shape=(out, out),
-        in_specs=[smem, smem, vmem, vmem, vmem],
+        in_specs=[smem, smem] + [pl.BlockSpec(memory_space=pl.ANY)] * 3,
         out_specs=(vmem, vmem),
         scratch_shapes=[
             pltpu.VMEM((n_bra, cols, width, flat), half),
@@ -258,6 +266,9 @@
             pltpu.VMEM((away, width, flat), half),
             pltpu.VMEM((n_ket, cols, dens_count, points), single),
             pltpu.VMEM((n_ket - 1, cols, dens_count, points), single),
+            pltpu.VMEM((blocks, width, points), half),
+            pltpu.VMEM((points, points), single),
+            dma((3,)),
             pltpu.VMEM((blocks, points, -(-named * padded // 128) * 128), half),
             pltpu.SMEM((blocks, named), jnp.int32),
             pltpu.SMEM((blocks, named), jnp.int32),

time: 37.9 us -> 37.8 us (level)
  no operation moved by 1% of the time
where the time goes in v5:
time: 37.8 us; the launch traced here: 37.6 us
  Pallas kernels  34.1 us (90%)
  local copies, waits for them, and re-layouts  2.23 us (6%)
  between operations  1.29 us (3%)
    pallas_call x1, Pallas kernels, per_device(): pl.pallas_call(functools.partial(kernel, dims), out_shape=(out, out), in_...  34.1 us
    unnamed x4, local copies, waits for them, and re-layouts  2.23 us

profile of v5, /device:TPU:0, one launch (start us, length us, event | category | flops | bytes accessed | tf_op | source)
XLA Modules:
  0.0 37.6 jit_solution(4909501548113642208)
XLA Ops:
  1.3 34.1 %shard_map.68 = (bf16[2,40,640]{2,1,0:T(8,128)(2,1)}, bf16[2,40,640]{2,1,0:T(8,128)(2,1)}) custom-call(s32[1,3,1,16]{3,2,1,0:T(1,128)} %bitcast.7, s32[1,1]{1,0:T(1,128)S(6)} %copy.9.live_ref, bf16[2,40,640]{2,1,0:T(8,128)(2,1)} %bitcast.6, bf16[8,40,256]{2,1,0:T(8,128)(2,1)} %fit_hbm.1, f32[256,256]{1,0:T(8,128)} %coup_hbm.1), custom_call_target="tpu_custom_call" | custom-call | tf_op jit(solution)/shard_map/pallas_call | solution.py:252
  35.4 0.0 copy-start
  35.4 1.6 %copy.10 = bf16[1,2,40,640]{3,2,1,0:T(8,128)(2,1)} copy(bf16[1,2,40,640]{3,2,1,0:T(8,128)(2,1)} %bitcast.5) | data formatting | bytes 204800
  37.0 0.0 copy-done
  37.0 0.6 %copy.11 = bf16[1,2,40,640]{3,2,1,0:T(8,128)(2,1)} copy(bf16[1,2,40,640]{3,2,1,0:T(8,128)(2,1)S(1)} %bitcast.4) | data formatting | bytes 204800
Async XLA Ops:
  35.4 1.6 %copy-start = (bf16[2,40,640]{2,1,0:T(8,128)(2,1)S(1)}, bf16[2,40,640]{2,1,0:T(8,128)(2,1)}, u32[]{:S(2)}) copy-start(bf16[2,40,640]{2,1,0:T(8,128)(2,1)} %get-tuple-element.5) | copy-start | bytes 307204
